TPU v7x, 32 devices: a whole 2x2x4 slice. The times are simulated.
32 devices in a mesh: row: 16 (over z, y, core), col: 2 (over x).
Axes of the slice: x: 2, y: 2, z: 4, core: 2. Of those that a mesh axis runs over, the one named last changes fastest.
Arguments:
- damping: bfloat16 [1536, 128, 1536], P('col', 'row'), may hold values from -60 to 60
- block_seeds: int32 [32], replicated, may hold values from 1 to 65520
Outputs:
- basis: float32 [32, 1536, 32], P('row', 'col')
All inputs are finite; a program needn't handle non-finite values.
Results may differ from a plain program's by a relative error of at most 0.0057.
Values may be sent and summed in bfloat16 or wider, within the bound.
No kernel may reach another device: no remote copies, remote signals or barrier semaphores. Data moves between devices by JAX's collectives and lax.ppermute only.
A program may use at most 192 MiB of HBM per device.

v0:
```python
import math
import jax
import jax.numpy as jnp
from jax import lax
from jax.sharding import PartitionSpec as P

NF = 128
M = 1536
P_SIZE = 32
NB = 32
NSTEPS = 12


def lag_table():
    lag_idx = jnp.arange(2 * NB, dtype=jnp.float32)[:, None]
    freq_idx = jnp.arange(NF, dtype=jnp.float32)[None, :]
    window = jnp.exp(-math.log(3.0) * lag_idx / NB)
    cos_table = (
        jnp.cos(math.pi * (freq_idx + 0.5) * lag_idx / NF)
        * window
        * math.sqrt(2.0 / NF)
        / math.sqrt(NB * M)
    )
    return cos_table.astype(jnp.bfloat16)


def probe_blocks(block_seeds, start_col, number):
    prime_mod = 65521
    column = (start_col + jnp.arange(number, dtype=jnp.int32))[None, :, None]
    probe_col = jnp.arange(P_SIZE, dtype=jnp.int32)[None, None, :]
    seed_col = block_seeds[:, None, None]
    inner_part = seed_col * (column + 1) % prime_mod * (column + 3) % prime_mod
    phase_val = (
        inner_part * (probe_col + 1) + seed_col * (probe_col + 1) % prime_mod * (probe_col + 2)
    ) % prime_mod
    return jnp.cos(2.0 * math.pi * phase_val.astype(jnp.float32) / prime_mod).astype(jnp.bfloat16)


def hankel_stack(blocks, group_len):
    extent = blocks.shape[0] + group_len - 1
    padded = jnp.pad(blocks, ((group_len - 1, group_len - 1), (0, 0), (0, 0)))
    shifted = [
        padded[group_len - 1 - offset : group_len - 1 - offset + extent]
        for offset in range(group_len)
    ]
    return jnp.stack(shifted, axis=2).reshape(extent, blocks.shape[1], group_len * blocks.shape[2])


def hankel_pass(lag_tiles, stack, shift_by, form, group_len):
    extent = stack.shape[0]
    pieces = []
    for group in range(NB // group_len):
        start_lag = group * group_len + shift_by
        window_lags = lag_tiles[start_lag : start_lag + extent]
        product = jnp.einsum(form, window_lags, stack, preferred_element_type=jnp.float32)
        pieces.append(product.reshape(product.shape[0], group_len, P_SIZE).transpose(1, 0, 2))
    return jnp.concatenate(pieces, axis=0)


def gram_of(blocks):
    return jnp.einsum("bcp,bcq->pq", blocks, blocks, precision=lax.Precision.HIGHEST)


def finish(mine, gram):
    highest = lax.Precision.HIGHEST
    scale = jnp.trace(gram) + 1e-06
    current = gram / scale
    eye_mat = jnp.eye(P_SIZE, dtype=jnp.float32)
    inverse = eye_mat
    for repeat in range(NSTEPS):
        weight = 1.5 * eye_mat - 0.5 * jnp.dot(inverse, current, precision=highest)
        current = jnp.dot(current, weight, precision=highest)
        inverse = jnp.dot(weight, inverse, precision=highest)
    factor = math.sqrt(NB * M) / jnp.sqrt(scale)
    return factor * jnp.einsum("bcp,pq->bcq", mine, inverse, precision=highest)


def shards(damping, block_seeds):
    group_len = min(16, NB)
    tile_cols = damping.shape[0]
    cos_table = lag_table()
    lag_tiles = jnp.einsum(
        "lk,nkr->lrn",
        cos_table,
        lax.all_to_all(damping, "row", split_axis=2, concat_axis=1, tiled=True),
        preferred_element_type=jnp.float32,
    ).astype(jnp.bfloat16)
    local_probes = probe_blocks(block_seeds, lax.axis_index("col") * tile_cols, tile_cols)
    partial_rows = hankel_pass(
        lag_tiles, hankel_stack(local_probes, group_len), 0, "lrc,lcn->rn", group_len
    )
    forward_b = lax.psum(partial_rows, "col").astype(jnp.bfloat16)
    partial_cols = hankel_pass(
        lag_tiles, hankel_stack(forward_b, group_len), 1, "lrc,lrn->cn", group_len
    )
    mine = lax.psum_scatter(partial_cols, "row", scatter_dimension=0, tiled=True)
    gram = lax.psum(gram_of(mine), ("row", "col"))
    return finish(mine, gram)


def solution(mesh):
    return jax.shard_map(
        shards,
        mesh=mesh,
        in_specs=(P("col", "row", None), P()),
        out_specs=P("row", "col", None),
        check_vma=False,
    )
```

profile of v0, /device:TPU:0, one launch (start us, length us, event | category | flops | bytes accessed | tf_op | source)
XLA Modules:
  0.0 698.7 jit_solution(12683558152289276993)
XLA Ops:
  6.5 26.8 %copy.35 = bf16[768,8,1536]{0,1,2:T(8,128)(2,1)} copy(bf16[768,8,1536]{2,1,0:T(8,128)(2,1)} %param.2) | data formatting | bytes 37748736 | tf_op args[0]
  33.3 7.6 %all-to-all-start = ((bf16[768,8,1536]{0,1,2:T(8,128)(2,1)}), bf16[768,8,1536]{0,1,2:T(8,128)(2,1)}, u32[]{:S(2)}, u32[]{:S(2)}) async-start(bf16[768,8,1536]{0,1,2:T(8,128)(2,1)} %copy.35), calls=%async_computation | async-start | bytes 37748736 | tf_op jit(solution)/shard_map/all_to_all | solution.py:85
  41.3 12.4 %fusion.23 = bf16[32,768,32]{1,2,0:T(8,128)(2,1)S(1)} fusion(s32[32,32]{1,0:T(8,128)S(1)} %fusion.133, s32[32]{0:T(128)S(1)} %get-tuple-element.10, s32[32,768]{1,0:T(8,128)S(1)} %add_select_fusion.1), kind=kLoop, calls=%fused_computation.39 | loop fusion | flops 8650752 | bytes 1675392 | tf_op jit(solution)/shard_map/convert_element_type | solution.py:36
  53.7 1.7 fusion.28
  55.4 1.7 fusion.30
  60.4 1.7 fusion.36
  62.1 1.7 fusion.38
  65.5 1.7 fusion.42
  67.2 1.7 fusion.44
  68.9 1.7 fusion.46
  77.3 1.7 fusion.56
  80.7 293.4 %all-to-all-done = bf16[768,8,1536]{0,1,2:T(8,128)(2,1)} async-done(((bf16[768,8,1536]{0,1,2:T(8,128)(2,1)}), bf16[768,8,1536]{0,1,2:T(8,128)(2,1)}, u32[]{:S(2)}, u32[]{:S(2)}) %all-to-all-start) | async-done | bytes 18874400 | tf_op jit(solution)/shard_map/all_to_all | solution.py:85
  374.1 18.7 %copy.37 = bf16[768,16,8,96]{0,3,2,1:T(8,128)(2,1)} copy(bf16[768,16,8,96]{0,2,3,1:T(8,128)(2,1)} %bitcast.41) | data formatting | bytes 37748736 | tf_op jit(solution)/shard_map/all_to_all | solution.py:85
  392.8 26.2 %convert_bitcast_fusion = bf16[64,96,768]{2,0,1:T(8,128)(2,1)S(1)} fusion(bf16[768,128,96]{0,2,1:T(8,128)(2,1)} %bitcast.321, f32[64]{0:T(128)S(1)} %multiply_exponential_fusion, f32[128]{0:T(128)S(1)} %add_multiply_fusion), kind=kOutput, calls=%fused_computation.6 | convolution fusion | flops 1212719104 | bytes 28312320 | tf_op jit(solution)/shard_map/lk,nkr->lrn/dot_general | solution.py:82
  419.0 8.6 %fusion.147 = (bf16[47,96,768]{2,0,1:T(8,128)(2,1)}, bf16[47,96,768]{2,0,1:T(8,128)(2,1)}, bf16[47,96,768]{2,0,1:T(8,128)(2,1)}, bf16[47,96,768]{2,0,1:T(8,128)(2,1)S(1)}) fusion(bf16[64,96,768]{2,0,1:T(8,128)(2,1)S(1)} %convert_bitcast_fusion), kind=kLoop, calls=%fused_computation.194 | loop fusion | bytes 55443456 | tf_op jit(solution)/shard_map/slice | solution.py:54
  427.6 22.3 %fusion.69 = f32[16,96,32]{1,2,0:T(8,128)S(1)} fusion(bf16[47,768,16,32]{1,3,2,0:T(8,128)(2,1)} %fusion.58, bf16[47,96,768]{2,0,1:T(8,128)(2,1)} %get-tuple-element.7), kind=kOutput, calls=%fused_computation.95 | convolution fusion | flops 3548381184 | bytes 44089344 | tf_op jit(solution)/shard_map/lrc,lcn->rn/dot_general | solution.py:55
  449.9 15.9 %fusion.74 = f32[16,96,32]{1,2,0:T(8,128)S(1)} fusion(bf16[47,768,16,32]{1,3,2,0:T(8,128)(2,1)} %fusion.58, bf16[47,96,768]{2,0,1:T(8,128)(2,1)S(1)} %get-tuple-element.8), kind=kOutput, calls=%fused_computation.96 | convolution fusion | flops 3548381184 | bytes 44089344 | tf_op jit(solution)/shard_map/lrc,lcn->rn/dot_general | solution.py:55
  465.9 19.4 %all-reduce.3 = bf16[32,96,32]{1,2,0:T(8,128)(2,1)S(1)} all-reduce(f32[32,96,32]{1,2,0:T(8,128)S(1)} %pad_maximum_fusion.1), channel_id=1, replica_groups=mesh['row'=16,'col'=2] {'col'}, use_global_device_ids=true, to_apply=%region_0.1 | all-reduce | flops 98304 | bytes 589824 | tf_op jit(solution)/shard_map/psum | solution.py:92
  486.8 8.5 %fusion.59 = f32[16,768,32]{1,2,0:T(8,128)S(1)} fusion(bf16[47,96,16,32]{1,3,0,2:T(8,128)(2,1)S(1)} %fusion.122, bf16[47,96,768]{2,0,1:T(8,128)(2,1)} %get-tuple-element.5), kind=kOutput, calls=%fused_computation.77 | convolution fusion | flops 3548381184 | bytes 13123584 | tf_op jit(solution)/shard_map/lrc,lrn->cn/dot_general | solution.py:55
  495.3 6.2 fusion.64
  501.5 1.9 pad_maximum_fusion
  503.4 138.3 %reduce-scatter.2.cloned.1.call-done = f32[2,768,32]{1,2,0:T(8,128)} async-done(((f32[32,768,32]{1,2,0:T(8,128)}), f32[2,768,32]{1,2,0:T(8,128)}) %reduce-scatter.2.cloned.1.call-update) | async-done | bytes 196624 | tf_op jit(solution)/shard_map/reduce_scatter | solution.py:96
  643.1 39.8 %psum.15 = f32[32,32]{1,0:T(8,128)S(1)} all-reduce(f32[32,32]{1,0:T(8,128)S(1)} %convolution_bitcast_fusion.1), channel_id=1, replica_groups=mesh['row'=16,'col'=2] {'row','col'}, use_global_device_ids=true, to_apply=%region_2.3 | all-reduce | flops 1024 | bytes 8192 | tf_op jit(solution)/shard_map/psum | solution.py:97
  689.6 1.9 convolution_multiply_fusion
  (77 shorter events, 22.4 us)
Async XLA Ops:
  33.3 7.7 %copy-start = (s32[32]{0:T(128)S(1)}, s32[32]{0:T(128)}, u32[]{:S(2)}) copy-start(s32[32]{0:T(128)} %param.3) | copy-start | bytes 388
  33.3 340.8 %all-to-all-start = ((bf16[768,8,1536]{0,1,2:T(8,128)(2,1)}), bf16[768,8,1536]{0,1,2:T(8,128)(2,1)}, u32[]{:S(2)}, u32[]{:S(2)}) async-start(bf16[768,8,1536]{0,1,2:T(8,128)(2,1)} %copy.35), calls=%async_computation | async-start | bytes 37748736 | tf_op jit(solution)/shard_map/all_to_all | solution.py:85
  40.9 600.8 %reduce-scatter.2.cloned.1.call-start = ((), (), s32[]{:S(2)}) async-start(), calls=%async_computation.2 | async-start | bytes 3342336 | tf_op jit(solution)/shard_map/reduce_scatter | solution.py:96
  486.3 9.0 %slice-start = ((s8[7077888]{0:T(1024)(128)(4,1)}), s8[4194304]{0:T(1024)(128)(4,1)S(1)}, s32[]{:S(2)}) async-start(s8[7077888]{0:T(1024)(128)(4,1)} %bitcast.322), calls=%async_computation.3 | async-start | bytes 8388608
  486.8 8.5 %slice-start.1 = ((s8[7077888]{0:T(1024)(128)(4,1)}), s8[2883584]{0:T(1024)(128)(4,1)S(1)}, s32[]{:S(2)}) async-start(s8[7077888]{0:T(1024)(128)(4,1)} %bitcast.322), calls=%async_computation.4 | async-start | bytes 5767168
Sparse Core Ops, SparseCore 0:
  503.5 138.1 reduce-scatter.1
where the time goes:
time: 706 us; the launch traced here: 699 us
  waiting for transfers between devices  432 us (61%)
  matrix products  87.6 us (12%)
  local copies, waits for them, and re-layouts  82.6 us (12%)
  blocking collectives  59.2 us (8%)
  other arithmetic  15.2 us (2%)
  between operations  14.8 us (2%)
  starting transfers between devices  7.63 us (1%)
    all_to_all x1, waiting for transfers between devices, shards(): lax.all_to_all(damping, 'row', split_axis=2, concat_axis=1, tiled=True)  293 us
    reduce_scatter x1, waiting for transfers between devices, shards(): lax.psum_scatter(partial_cols, 'row', scatter_dimension=0, tiled=True)  138 us
    unnamed x37, local copies, waits for them, and re-layouts  53.5 us
    dot_general x4, matrix products, hankel_pass(): jnp.einsum(form, window_lags, stack, preferred_element_type=jnp.float32)  52.9 us
    psum x1, blocking collectives, shards(): gram = lax.psum(gram_of(mine), ('row', 'col'))  39.8 us
    dot_general x1, matrix products, shards(): jnp.einsum('lk,nkr->lrn', cos_table, lax.all_to_all(damping, 'row', split...  26.2 us
    psum x1, blocking collectives, shards(): forward_b = lax.psum(partial_rows, 'col').astype(jnp.bfloat16)  19.4 us
    all_to_all x1, local copies, waits for them, and re-layouts, shards(): lax.all_to_all(damping, 'row', split_axis=2, concat_axis=1, tiled=True)  18.7 us
  transfers between devices with their start and end apart: 2, of which 2 were waited for; matrix products, arithmetic and copies ran while one was open for 6% of the time, Pallas kernels for 0%

commit v1 on v0

--- a/solution.py
+++ b/solution.py
@@ -94,7 +94,7 @@
         lag_tiles, hankel_stack(forward_b, group_len), 1, "lrc,lrn->cn", group_len
     )
     mine = lax.psum_scatter(partial_cols, "row", scatter_dimension=0, tiled=True)
-    gram = lax.psum(gram_of(mine), ("row", "col"))
+    gram = jnp.sum(lax.all_gather(gram_of(mine), ("row", "col")), axis=0)
     return finish(mine, gram)
 
 

time: 706 us -> 731 us (1.035)
  blocking collectives: 59.2 us -> 87 us
    all_gather x0 -> x1, blocking collectives: none -> 67.7 us  [shards(): gram = jnp.sum(lax.all_gather(gram_of(mine), ('row', 'col')), axis=0)]
    psum x1 -> x0, blocking collectives: 39.8 us -> none  [shards(): gram = lax.psum(gram_of(mine), ('row', 'col'))]
    dot_general x1, matrix products: 26.2 us -> 15.6 us  [shards(): jnp.einsum('lk,nkr->lrn', cos_table, lax.all_to_all(damping, 'row', split...]
    dot_general x4, matrix products: 52.9 us -> 60.9 us  [hankel_pass(): jnp.einsum(form, window_lags, stack, preferred_element_type=jnp.float32)]
  transfers between devices with their start and end apart: 2 -> 2, of which waited for: 2 -> 2; matrix products, arithmetic and copies ran while one was open for 6% -> 5% of each run, Pallas kernels for 0% -> 0%
where the time goes in v1:
time: 731 us; the launch traced here: 724 us
  waiting for transfers between devices  432 us (59%)
  blocking collectives  87 us (12%)
  matrix products  85 us (12%)
  local copies, waits for them, and re-layouts  82.6 us (11%)
  other arithmetic  15.3 us (2%)
  between operations  14.4 us (2%)
  starting transfers between devices  7.63 us (1%)
    all_to_all x1, waiting for transfers between devices, shards(): lax.all_to_all(damping, 'row', split_axis=2, concat_axis=1, tiled=True)  293 us
    reduce_scatter x1, waiting for transfers between devices, shards(): lax.psum_scatter(partial_cols, 'row', scatter_dimension=0, tiled=True)  138 us
    all_gather x1, blocking collectives, shards(): gram = jnp.sum(lax.all_gather(gram_of(mine), ('row', 'col')), axis=0)  67.7 us
    dot_general x4, matrix products, hankel_pass(): jnp.einsum(form, window_lags, stack, preferred_element_type=jnp.float32)  60.9 us
    unnamed x37, local copies, waits for them, and re-layouts  53.5 us
    psum x1, blocking collectives, shards(): forward_b = lax.psum(partial_rows, 'col').astype(jnp.bfloat16)  19.4 us
    all_to_all x1, local copies, waits for them, and re-layouts, shards(): lax.all_to_all(damping, 'row', split_axis=2, concat_axis=1, tiled=True)  18.7 us
    dot_general x1, matrix products, shards(): jnp.einsum('lk,nkr->lrn', cos_table, lax.all_to_all(damping, 'row', split...  15.6 us
  transfers between devices with their start and end apart: 2, of which 2 were waited for; matrix products, arithmetic and copies ran while one was open for 5% of the time, Pallas kernels for 0%

profile of v1, /device:TPU:0, one launch (start us, length us, event | category | flops | bytes accessed | tf_op | source)
XLA Modules:
  0.0 723.7 jit_solution(11959176674104294575)
XLA Ops:
  6.5 26.8 %copy.35 = bf16[768,8,1536]{0,1,2:T(8,128)(2,1)} copy(bf16[768,8,1536]{2,1,0:T(8,128)(2,1)} %param.2) | data formatting | bytes 37748736 | tf_op args[0]
  33.3 7.6 %all-to-all-start = ((bf16[768,8,1536]{0,1,2:T(8,128)(2,1)}), bf16[768,8,1536]{0,1,2:T(8,128)(2,1)}, u32[]{:S(2)}, u32[]{:S(2)}) async-start(bf16[768,8,1536]{0,1,2:T(8,128)(2,1)} %copy.35), calls=%async_computation | async-start | bytes 37748736 | tf_op jit(solution)/shard_map/all_to_all | solution.py:85
  41.3 12.4 %fusion.23 = bf16[32,768,32]{1,2,0:T(8,128)(2,1)S(1)} fusion(s32[32,32]{1,0:T(8,128)S(1)} %fusion.133, s32[32]{0:T(128)S(1)} %get-tuple-element.10, s32[32,768]{1,0:T(8,128)S(1)} %add_select_fusion.1), kind=kLoop, calls=%fused_computation.39 | loop fusion | flops 8650752 | bytes 1675392 | tf_op jit(solution)/shard_map/convert_element_type | solution.py:36
  53.7 1.7 fusion.28
  55.4 1.7 fusion.30
  60.4 1.7 fusion.36
  62.1 1.7 fusion.38
  65.5 1.7 fusion.42
  67.2 1.7 fusion.44
  68.9 1.7 fusion.46
  77.3 1.7 fusion.56
  80.7 293.4 %all-to-all-done = bf16[768,8,1536]{0,1,2:T(8,128)(2,1)} async-done(((bf16[768,8,1536]{0,1,2:T(8,128)(2,1)}), bf16[768,8,1536]{0,1,2:T(8,128)(2,1)}, u32[]{:S(2)}, u32[]{:S(2)}) %all-to-all-start) | async-done | bytes 18874400 | tf_op jit(solution)/shard_map/all_to_all | solution.py:85
  374.1 18.7 %copy.37 = bf16[768,16,8,96]{0,3,2,1:T(8,128)(2,1)} copy(bf16[768,16,8,96]{0,2,3,1:T(8,128)(2,1)} %bitcast.41) | data formatting | bytes 37748736 | tf_op jit(solution)/shard_map/all_to_all | solution.py:85
  392.8 15.6 %convert_bitcast_fusion = bf16[64,96,768]{2,0,1:T(8,128)(2,1)S(1)} fusion(bf16[768,128,96]{0,2,1:T(8,128)(2,1)} %bitcast.322, f32[64]{0:T(128)S(1)} %multiply_exponential_fusion, f32[128]{0:T(128)S(1)} %add_multiply_fusion), kind=kOutput, calls=%fused_computation.6 | convolution fusion | flops 1212719104 | bytes 28312320 | tf_op jit(solution)/shard_map/lk,nkr->lrn/dot_general | solution.py:82
  408.4 8.6 %fusion.147 = (bf16[47,96,768]{2,0,1:T(8,128)(2,1)}, bf16[47,96,768]{2,0,1:T(8,128)(2,1)}, bf16[47,96,768]{2,0,1:T(8,128)(2,1)}, bf16[47,96,768]{2,0,1:T(8,128)(2,1)S(1)}) fusion(bf16[64,96,768]{2,0,1:T(8,128)(2,1)S(1)} %convert_bitcast_fusion), kind=kLoop, calls=%fused_computation.194 | loop fusion | bytes 55443456 | tf_op jit(solution)/shard_map/slice | solution.py:54
  417.0 22.3 %fusion.69 = f32[16,96,32]{1,2,0:T(8,128)S(1)} fusion(bf16[47,768,16,32]{1,3,2,0:T(8,128)(2,1)} %fusion.58, bf16[47,96,768]{2,0,1:T(8,128)(2,1)} %get-tuple-element.7), kind=kOutput, calls=%fused_computation.95 | convolution fusion | flops 3548381184 | bytes 44089344 | tf_op jit(solution)/shard_map/lrc,lcn->rn/dot_general | solution.py:55
  439.3 15.9 %fusion.74 = f32[16,96,32]{1,2,0:T(8,128)S(1)} fusion(bf16[47,768,16,32]{1,3,2,0:T(8,128)(2,1)} %fusion.58, bf16[47,96,768]{2,0,1:T(8,128)(2,1)S(1)} %get-tuple-element.8), kind=kOutput, calls=%fused_computation.96 | convolution fusion | flops 3548381184 | bytes 44089344 | tf_op jit(solution)/shard_map/lrc,lcn->rn/dot_general | solution.py:55
  455.3 19.4 %all-reduce.3 = bf16[32,96,32]{1,2,0:T(8,128)(2,1)S(1)} all-reduce(f32[32,96,32]{1,2,0:T(8,128)S(1)} %pad_maximum_fusion.1), channel_id=1, replica_groups=mesh['row'=16,'col'=2] {'col'}, use_global_device_ids=true, to_apply=%region_0.1 | all-reduce | flops 98304 | bytes 589824 | tf_op jit(solution)/shard_map/psum | solution.py:92
  476.2 16.5 %fusion.59 = f32[16,768,32]{1,2,0:T(8,128)S(1)} fusion(bf16[47,96,16,32]{1,3,0,2:T(8,128)(2,1)S(1)} %fusion.122, bf16[47,96,768]{2,0,1:T(8,128)(2,1)} %get-tuple-element.5), kind=kOutput, calls=%fused_computation.77 | convolution fusion | flops 3548381184 | bytes 13123584 | tf_op jit(solution)/shard_map/lrc,lrn->cn/dot_general | solution.py:55
  492.7 6.2 fusion.64
  498.9 1.9 pad_maximum_fusion
  500.8 138.4 %reduce-scatter.2.cloned.1.call-done = f32[2,768,32]{1,2,0:T(8,128)} async-done(((f32[32,768,32]{1,2,0:T(8,128)}), f32[2,768,32]{1,2,0:T(8,128)}) %reduce-scatter.2.cloned.1.call-update) | async-done | bytes 196624 | tf_op jit(solution)/shard_map/reduce_scatter | solution.py:96
  640.5 67.7 %all-gather = f32[1024,32]{1,0:T(8,128)S(1)} all-gather(f32[32,32]{1,0:T(8,128)S(1)} %convolution_bitcast_fusion.1), channel_id=2, replica_groups=mesh['row'=16,'col'=2] {'row','col'}, dimensions={0}, use_global_device_ids=true | all-gather | bytes 135168 | tf_op jit(solution)/shard_map/all_gather | solution.py:97
  714.9 1.9 convolution_multiply_fusion
  (78 shorter events, 22.5 us)
Async XLA Ops:
  33.3 7.7 %copy-start = (s32[32]{0:T(128)S(1)}, s32[32]{0:T(128)}, u32[]{:S(2)}) copy-start(s32[32]{0:T(128)} %param.3) | copy-start | bytes 388
  33.3 340.8 %all-to-all-start = ((bf16[768,8,1536]{0,1,2:T(8,128)(2,1)}), bf16[768,8,1536]{0,1,2:T(8,128)(2,1)}, u32[]{:S(2)}, u32[]{:S(2)}) async-start(bf16[768,8,1536]{0,1,2:T(8,128)(2,1)} %copy.35), calls=%async_computation | async-start | bytes 37748736 | tf_op jit(solution)/shard_map/all_to_all | solution.py:85
  40.9 598.3 %reduce-scatter.2.cloned.1.call-start = ((), (), s32[]{:S(2)}) async-start(), calls=%async_computation.2 | async-start | bytes 3342336 | tf_op jit(solution)/shard_map/reduce_scatter | solution.py:96
  475.7 17.0 %slice-start = ((s8[7077888]{0:T(1024)(128)(4,1)}), s8[4194304]{0:T(1024)(128)(4,1)S(1)}, s32[]{:S(2)}) async-start(s8[7077888]{0:T(1024)(128)(4,1)} %bitcast.323), calls=%async_computation.3 | async-start | bytes 8388608
  476.2 16.5 %slice-start.1 = ((s8[7077888]{0:T(1024)(128)(4,1)}), s8[2883584]{0:T(1024)(128)(4,1)S(1)}, s32[]{:S(2)}) async-start(s8[7077888]{0:T(1024)(128)(4,1)} %bitcast.323), calls=%async_computation.4 | async-start | bytes 5767168
Sparse Core Ops, SparseCore 0:
  500.9 138.1 reduce-scatter.1
